TPU v7x, 32 devices: a whole 2x2x4 slice. The times are simulated.
32 devices in a mesh: dp: 4 (over x, core), mp: 8 (over z, y).
Axes of the slice: x: 2, y: 2, z: 4, core: 2. Of those that a mesh axis runs over, the one named last changes fastest.
Arguments:
- block_input: bfloat16 [4096, 2048], P(('dp', 'mp')), may hold values from -6 to 6
- out_cotangent: bfloat16 [4096, 2048], P(('dp', 'mp')), may hold values from -6 to 6
- segments: int32 [4, 1024], P('dp'), may hold values from 0 to 3, never falling along the last dimension, each value on 1 to 512 neighbouring positions
- domain_tags: int32 [4], P('dp'), may hold values from 0 to 7
- counts: int32 [8], replicated, may hold values from 1 to 4
- attn_gain: float32 [2048], replicated, may hold values from 0.5 to 1.5
- mlp_gain: float32 [2048], replicated, may hold values from 0.5 to 1.5
- norm_gain: float32 [2048], P('mp'), may hold values from 0.5 to 1.5
- bound_table: float32 [24, 2048], P(None, 'mp'), may hold values from -4 to 4
- w_input: bfloat16 [2048, 2048], P(None, 'mp'), may hold values from -0.125 to 0.125
- w_forget: bfloat16 [2048, 2048], P(None, 'mp'), may hold values from -0.125 to 0.125
- w_gate_mix: bfloat16 [2048, 2048], P(None, 'mp'), may hold values from -0.125 to 0.125
- w_out: bfloat16 [2048, 2048], P('mp'), may hold values from -0.1875 to 0.1875
- w_glu_gate: bfloat16 [2048, 5632], P(None, 'mp'), may hold values from -0.125 to 0.125
- w_glu_up: bfloat16 [2048, 5632], P(None, 'mp'), may hold values from -0.125 to 0.125
- w_glu_down: bfloat16 [5632, 2048], P('mp'), may hold values from -0.109375 to 0.109375
Outputs:
- result: bfloat16 [4096, 2048], P(('dp', 'mp'))
- grad_block_input: float32 [4096, 2048], P(('dp', 'mp'))
- grad_attn_gain: float32 [2048], replicated
- grad_mlp_gain: float32 [2048], replicated
- grad_norm_gain: float32 [2048], replicated
- grad_bound_table: float32 [24, 2048], replicated
- grad_input: float32 [2048, 2048], P('dp', 'mp')
- grad_forget: float32 [2048, 2048], P('dp', 'mp')
- grad_gate_mix: float32 [2048, 2048], P('dp', 'mp')
- grad_out: float32 [2048, 2048], P('mp', 'dp')
- grad_glu_gate: float32 [2048, 5632], P('dp', 'mp')
- grad_glu_up: float32 [2048, 5632], P('dp', 'mp')
- grad_glu_down: float32 [5632, 2048], P('mp', 'dp')
Inputs may be any that keep to these rules, and one draw needn't show every extreme that they name: `segments`: along each row the document ids never fall; each document has at least one position.
All inputs are finite; a program needn't handle non-finite values.
Results may differ from a plain program's by a relative error of at most 0.022.
Values may be sent and summed in bfloat16 or wider, within the bound.
No kernel may reach another device: no remote copies, remote signals or barrier semaphores. Data moves between devices by JAX's collectives and lax.ppermute only.
A program may use at most 320 MiB of HBM per device.

v0:
```python
import jax
import jax.numpy as jnp
from jax import lax
from jax.sharding import PartitionSpec as P

NLAYER = 24
LAYER = 20
LEN = 1024
BLK = 128
NDOM = 8
EPS = 1e-06
HIGH = lax.Precision.HIGHEST


def inverse_rms(rows):
    return lax.rsqrt(jnp.mean(rows * rows, axis=1, keepdims=True) + EPS)


def silu_slope(value):
    sig = jax.nn.sigmoid(value)
    return sig * (1.0 + value * (1.0 - sig))


def norm_back(grad_normed, rows, inverse, gain):
    scaled = grad_normed * gain
    unit = rows * inverse
    back = inverse * (scaled - unit * jnp.mean(scaled * unit, axis=1, keepdims=True))
    return (back, jnp.sum(grad_normed * unit, axis=0))


def block_terms(log_blk, reset_blk, lower):
    cum_log = jnp.einsum("csu,tu->cst", log_blk, lower, precision=HIGH)
    cum_reset = jnp.einsum("su,tu->st", reset_blk, lower, precision=HIGH)
    same = (cum_reset[:, :, None] == cum_reset[:, None, :]) & (lower[None] > 0.5)
    spread = jnp.minimum(cum_log[:, :, :, None] - cum_log[:, :, None, :], 0.0)
    weight = jnp.where(same[None], jnp.exp(spread), 0.0)
    return (weight, cum_log, cum_reset)


def local(
    block_input,
    out_cotangent,
    segments,
    domain_tags,
    counts,
    attn_gain,
    mlp_gain,
    norm_gain,
    bound_table,
    w_input,
    w_forget,
    w_gate_mix,
    w_out,
    w_glu_gate,
    w_glu_up,
    w_glu_down,
):
    rows_dev, width = block_input.shape
    chans = w_input.shape[1]
    units = w_glu_gate.shape[1]
    seqs = segments.shape[0]
    total_rows = seqs * LEN
    nblk = LEN // BLK
    mp_index = lax.axis_index("mp")
    own_start = mp_index * rows_dev
    own_rows = block_input.astype(jnp.float32)
    own_inv1 = inverse_rms(own_rows)
    input_all = lax.all_gather(block_input, "mp", axis=0, tiled=True)
    input_all_f = input_all.astype(jnp.float32)
    normed_all = (input_all_f * inverse_rms(input_all_f) * attn_gain).astype(jnp.bfloat16)
    w_mix = jnp.concatenate([w_input, w_forget, w_gate_mix], axis=1)
    pre_mix = jnp.einsum("td,dc->ct", normed_all, w_mix, preferred_element_type=jnp.float32)
    pre_i = pre_mix[:chans].reshape(chans, seqs, LEN)
    pre_f = pre_mix[chans : 2 * chans].reshape(chans, seqs, LEN)
    pre_g = pre_mix[2 * chans :]
    shares = jax.nn.softmax(bound_table, axis=0)
    layer_ids = jnp.arange(NLAYER)
    pick = ((layer_ids >= 1) & (layer_ids <= LAYER)).astype(jnp.float32)[:, None]
    bound_vec = jnp.sum(shares * pick, axis=0)
    bound = bound_vec[:, None, None]
    sig_f = jax.nn.sigmoid(pre_f)
    forget = bound + (1.0 - bound) * sig_f
    act_i = jax.nn.silu(pre_i)
    update = act_i * (1.0 - forget)
    keep = jnp.concatenate(
        [
            jnp.zeros((seqs, 1), jnp.float32),
            (segments[:, 1:] == segments[:, :-1]).astype(jnp.float32),
        ],
        axis=1,
    )
    positions = jnp.arange(BLK)
    lower = (positions[None, :] <= positions[:, None]).astype(jnp.float32)

    def split_blocks(arr):
        arr = arr.reshape(arr.shape[:-1] + (nblk, BLK))
        return jnp.moveaxis(arr, -2, 0)

    def join_blocks(arr):
        arr = jnp.moveaxis(arr, 0, -2)
        return arr.reshape(arr.shape[:-2] + (LEN,))

    log_blocks = split_blocks(jnp.log(forget))
    reset_blocks = split_blocks(1.0 - keep)

    def forward_step(state, blk):
        log_blk, reset_blk, update_blk = blk
        weight, cum_log, cum_reset = block_terms(log_blk, reset_blk, lower)
        lead = jnp.where(cum_reset[None] == 0.0, jnp.exp(cum_log), 0.0)
        states_blk = (
            jnp.einsum("cstu,csu->cst", weight, update_blk, precision=HIGH)
            + lead * state[:, :, None]
        )
        return (states_blk[:, :, -1], states_blk)

    _, state_blocks = lax.scan(
        forward_step,
        jnp.zeros((chans, seqs), jnp.float32),
        (log_blocks, reset_blocks, split_blocks(update)),
    )
    states3 = join_blocks(state_blocks)
    states = states3.reshape(chans, total_rows)
    square_sum = lax.psum(jnp.sum(states * states, axis=0), "mp")
    rec_inv = lax.rsqrt(square_sum / width + EPS)
    unit_states = states * rec_inv[None, :]
    act_g = jax.nn.silu(pre_g)
    gated = (unit_states * norm_gain[:, None] * act_g).astype(jnp.bfloat16)
    partial_mix = jnp.einsum("ct,cd->td", gated, w_out, preferred_element_type=jnp.float32)
    middle_all = input_all_f + lax.psum(partial_mix.astype(jnp.bfloat16), "mp").astype(jnp.float32)
    normed_two_all = (middle_all * inverse_rms(middle_all) * mlp_gain).astype(jnp.bfloat16)
    middle = lax.dynamic_slice_in_dim(middle_all, own_start, rows_dev, 0)
    own_inv2 = inverse_rms(middle)
    w_glu = jnp.concatenate([w_glu_gate, w_glu_up], axis=1)
    gate_up = jnp.dot(normed_two_all, w_glu, preferred_element_type=jnp.float32)
    gate = gate_up[:, :units]
    up = gate_up[:, units:]
    act_gate = jax.nn.silu(gate)
    hidden = (act_gate * up).astype(jnp.bfloat16)
    piece = hidden
    final = middle + lax.psum_scatter(
        jnp.dot(piece, w_glu_down, preferred_element_type=jnp.float32).astype(jnp.bfloat16),
        "mp",
        scatter_dimension=0,
        tiled=True,
    ).astype(jnp.float32)
    result = final.astype(jnp.bfloat16)
    domain_hit = (domain_tags[:, None] == jnp.arange(NDOM)[None, :]).astype(jnp.float32)
    seq_count = jnp.dot(domain_hit, counts.astype(jnp.float32)[:, None], precision=HIGH)[:, 0]
    seq_weight = lax.rsqrt(seq_count)
    cot_all = lax.all_gather(out_cotangent, "mp", axis=0, tiled=True)
    grad_all = (
        cot_all.astype(jnp.float32).reshape(seqs, LEN, width) * seq_weight[:, None, None]
    ).reshape(total_rows, width)
    grad_all_b = grad_all.astype(jnp.bfloat16)
    grad_own = lax.dynamic_slice_in_dim(grad_all, own_start, rows_dev, 0)
    grad_hidden = jnp.einsum(
        "td,fd->tf", grad_all_b, w_glu_down, preferred_element_type=jnp.float32
    )
    down_term = jnp.einsum("tf,td->fd", hidden, grad_all_b, preferred_element_type=jnp.float32)
    grad_gate = grad_hidden * up * silu_slope(gate)
    grad_up = grad_hidden * act_gate
    grad_gate_up = jnp.concatenate([grad_gate, grad_up], axis=1).astype(jnp.bfloat16)
    piece = grad_gate_up
    grad_normed_two = lax.psum_scatter(
        jnp.einsum("tf,df->td", piece, w_glu, preferred_element_type=jnp.float32).astype(
            jnp.bfloat16
        ),
        "mp",
        scatter_dimension=0,
        tiled=True,
    ).astype(jnp.float32)
    back_two, mlp_gain_term = norm_back(grad_normed_two, middle, own_inv2, mlp_gain)
    grad_middle = grad_own + back_two
    middle_grad_all = lax.all_gather(grad_middle.astype(jnp.bfloat16), "mp", axis=0, tiled=True)
    grad_gated = jnp.einsum("td,cd->ct", middle_grad_all, w_out, preferred_element_type=jnp.float32)
    out_term = jnp.einsum("ct,td->cd", gated, middle_grad_all, preferred_element_type=jnp.float32)
    grad_unit = grad_gated * norm_gain[:, None] * act_g
    norm_gain_term = jnp.sum(grad_gated * unit_states * act_g, axis=1)
    grad_pre_g = grad_gated * unit_states * norm_gain[:, None] * silu_slope(pre_g)
    inner = lax.psum(jnp.sum(grad_unit * unit_states, axis=0), "mp")
    grad_states = rec_inv[None, :] * (grad_unit - unit_states * (inner / width)[None, :])
    forget_heads = split_blocks(forget)[..., 0]
    keep_heads = split_blocks(keep)[..., 0]

    def backward_step(carry, blk):
        log_blk, reset_blk, grad_blk, forget_head, keep_head = blk
        weight, cum_log, cum_reset = block_terms(log_blk, reset_blk, lower)
        trailing = jnp.where(
            (cum_reset == cum_reset[:, -1:])[None], jnp.exp(cum_log[:, :, -1:] - cum_log), 0.0
        )
        total = (
            jnp.einsum("cstu,cst->csu", weight, grad_blk, precision=HIGH)
            + trailing * carry[:, :, None]
        )
        return (forget_head * keep_head[None] * total[:, :, 0], total)

    _, grad_blocks = lax.scan(
        backward_step,
        jnp.zeros((chans, seqs), jnp.float32),
        (
            log_blocks,
            reset_blocks,
            split_blocks(grad_states.reshape(chans, seqs, LEN)),
            forget_heads,
            keep_heads,
        ),
        reverse=True,
    )
    grad_update = join_blocks(grad_blocks)
    prior = jnp.concatenate([jnp.zeros((chans, seqs, 1), jnp.float32), states3[:, :, :-1]], axis=2)
    grad_forget = grad_update * keep[None] * prior - grad_update * act_i
    grad_pre_i = grad_update * (1.0 - forget) * silu_slope(pre_i)
    grad_pre_f = grad_forget * (1.0 - bound) * sig_f * (1.0 - sig_f)
    bound_grad = jnp.sum(grad_forget * (1.0 - sig_f), axis=(1, 2))
    pick_grad = pick * bound_grad[None, :]
    table_term = shares * (pick_grad - jnp.sum(shares * pick_grad, axis=0, keepdims=True))
    grad_pre = jnp.concatenate(
        [grad_pre_i.reshape(chans, total_rows), grad_pre_f.reshape(chans, total_rows), grad_pre_g],
        axis=0,
    ).astype(jnp.bfloat16)
    piece = grad_pre
    grad_normed = lax.psum_scatter(
        jnp.einsum("ct,dc->td", piece, w_mix, preferred_element_type=jnp.float32).astype(
            jnp.bfloat16
        ),
        "mp",
        scatter_dimension=0,
        tiled=True,
    ).astype(jnp.float32)
    back_one, attn_gain_term = norm_back(grad_normed, own_rows, own_inv1, attn_gain)
    grad_block_input = grad_middle + back_one
    mix_part = jnp.einsum("tk,ct->kc", normed_all, grad_pre, preferred_element_type=jnp.float32)
    glu_part = jnp.einsum(
        "tk,tf->kf", normed_two_all, grad_gate_up, preferred_element_type=jnp.float32
    )
    weight_grads = lax.psum_scatter(
        jnp.concatenate([mix_part, glu_part], axis=1).astype(jnp.bfloat16),
        "dp",
        scatter_dimension=0,
        tiled=True,
    ).astype(jnp.float32)
    out_grad, down_grad = (
        lax.psum_scatter(
            out_term.astype(jnp.bfloat16), "dp", scatter_dimension=1, tiled=True
        ).astype(jnp.float32),
        lax.psum_scatter(
            down_term.astype(jnp.bfloat16), "dp", scatter_dimension=1, tiled=True
        ).astype(jnp.float32),
    )
    groups = lax.axis_size("mp")
    onehot = (jnp.arange(groups) == mp_index).astype(jnp.float32)
    norm_full = (onehot[:, None] * norm_gain_term[None, :]).reshape(width)
    table_full = (table_term[:, None, :] * onehot[None, :, None]).reshape(NLAYER, width)
    attn_sum, mlp_sum, norm_sum, table_sum = lax.psum(
        (attn_gain_term, mlp_gain_term, norm_full, table_full), ("dp", "mp")
    )
    grad_input = weight_grads[:, :chans]
    grad_forget_w = weight_grads[:, chans : 2 * chans]
    grad_gate_mix = weight_grads[:, 2 * chans : 3 * chans]
    grad_glu_gate = weight_grads[:, 3 * chans : 3 * chans + units]
    grad_glu_up = weight_grads[:, 3 * chans + units :]
    return (
        result,
        grad_block_input,
        attn_sum,
        mlp_sum,
        norm_sum,
        table_sum,
        grad_input,
        grad_forget_w,
        grad_gate_mix,
        out_grad,
        grad_glu_gate,
        grad_glu_up,
        down_grad,
    )


def solution(mesh):
    placed = (
        P(("dp", "mp"), None),
        P(("dp", "mp"), None),
        P("dp", None),
        P("dp"),
        P(),
        P(),
        P(),
        P("mp"),
        P(None, "mp"),
        P(None, "mp"),
        P(None, "mp"),
        P(None, "mp"),
        P("mp", None),
        P(None, "mp"),
        P(None, "mp"),
        P("mp", None),
    )
    return jax.shard_map(
        local,
        mesh=mesh,
        in_specs=placed,
        out_specs=(
            P(("dp", "mp"), None),
            P(("dp", "mp"), None),
            P(),
            P(),
            P(),
            P(),
            P("dp", "mp"),
            P("dp", "mp"),
            P("dp", "mp"),
            P("mp", "dp"),
            P("dp", "mp"),
            P("dp", "mp"),
            P("mp", "dp"),
        ),
        check_vma=False,
    )
```

profile of v0, /device:TPU:10, one launch (start us, length us, event | category | flops | bytes accessed | tf_op | source)
XLA Modules:
  0.0 1434.1 jit_solution(5197083218827090929)
XLA Ops:
  17.3 66.8 %all-gather.4.cloned.1.call-done = bf16[1024,2048]{1,0:T(8,128)(2,1)} async-done(((bf16[128,2048]{1,0:T(8,128)(2,1)}), bf16[1024,2048]{1,0:T(8,128)(2,1)}) %all-gather.4.cloned.1.call-update) | async-done | bytes 4194320 | tf_op jit(solution)/shard_map/all_gather | solution.py:68
  87.5 5.6 fusion.61
  95.5 3.5 copy_bitcast_fusion.1
  100.1 259.9 %while.32 = (s32[]{:T(128)}, f32[256,1]{0,1:T(1,128)S(1)}, f32[8,256,1,128]{1,3,2,0:T(8,128)}, f32[8,1,128]{2,1,0:T(1,128)S(1)}, f32[8,256,1,128]{3,2,1,0:T(1,128)}, /*index=5*/f32[8,256,1,128]{3,2,1,0:T(1,128)}, s32[]{:T(128)}) while((s32[]{:T(128)}, f32[256,1]{0,1:T(1,128)S(1)}, f32[8,256,1,128]{1,3,2,0:T(8,128)}, ...), condition=%wide.region_5.6_spmd.clone.clone, body=%wide.region_4.0_spmd.clone.clone.sunk | while | flops 113787008 | bytes 2398181 | solution.py:116
  102.0 28.5 %fusion.137 = f32[256,1,128]{2,1,0:T(1,128)S(1)} fusion(f32[256,128]{1,0:T(8,128)S(1)} %copy.93, pred[128,128]{1,0:T(8,128)(4,1)S(1)} %fusion.136, f32[8,256,1,128]{3,2,1,0:T(1,128)} %get-tuple-element.526, s32[]{:T(128)S(6)} %copy.104), kind=kOutput, calls=%fused_computation.2.clone.1 | convolution fusion | flops 62914560 | bytes 540676 | tf_op jit(solution)/shard_map/while/body/eval_jaxpr/cstu,csu->cst/dot_general | solution.py:111
  133.1 28.5 %fusion.137 = f32[256,1,128]{2,1,0:T(1,128)S(1)} fusion(f32[256,128]{1,0:T(8,128)S(1)} %copy.93, pred[128,128]{1,0:T(8,128)(4,1)S(1)} %fusion.136, f32[8,256,1,128]{3,2,1,0:T(1,128)} %get-tuple-element.526, s32[]{:T(128)S(6)} %copy.104), kind=kOutput, calls=%fused_computation.2.clone.1 | convolution fusion | flops 62914560 | bytes 540676 | tf_op jit(solution)/shard_map/while/body/eval_jaxpr/cstu,csu->cst/dot_general | solution.py:111
  164.3 28.5 %fusion.137 = f32[256,1,128]{2,1,0:T(1,128)S(1)} fusion(f32[256,128]{1,0:T(8,128)S(1)} %copy.93, pred[128,128]{1,0:T(8,128)(4,1)S(1)} %fusion.136, f32[8,256,1,128]{3,2,1,0:T(1,128)} %get-tuple-element.526, s32[]{:T(128)S(6)} %copy.104), kind=kOutput, calls=%fused_computation.2.clone.1 | convolution fusion | flops 62914560 | bytes 540676 | tf_op jit(solution)/shard_map/while/body/eval_jaxpr/cstu,csu->cst/dot_general | solution.py:111
  195.4 28.5 %fusion.137 = f32[256,1,128]{2,1,0:T(1,128)S(1)} fusion(f32[256,128]{1,0:T(8,128)S(1)} %copy.93, pred[128,128]{1,0:T(8,128)(4,1)S(1)} %fusion.136, f32[8,256,1,128]{3,2,1,0:T(1,128)} %get-tuple-element.526, s32[]{:T(128)S(6)} %copy.104), kind=kOutput, calls=%fused_computation.2.clone.1 | convolution fusion | flops 62914560 | bytes 540676 | tf_op jit(solution)/shard_map/while/body/eval_jaxpr/cstu,csu->cst/dot_general | solution.py:111
  226.6 28.5 %fusion.137 = f32[256,1,128]{2,1,0:T(1,128)S(1)} fusion(f32[256,128]{1,0:T(8,128)S(1)} %copy.93, pred[128,128]{1,0:T(8,128)(4,1)S(1)} %fusion.136, f32[8,256,1,128]{3,2,1,0:T(1,128)} %get-tuple-element.526, s32[]{:T(128)S(6)} %copy.104), kind=kOutput, calls=%fused_computation.2.clone.1 | convolution fusion | flops 62914560 | bytes 540676 | tf_op jit(solution)/shard_map/while/body/eval_jaxpr/cstu,csu->cst/dot_general | solution.py:111
  257.7 28.5 %fusion.137 = f32[256,1,128]{2,1,0:T(1,128)S(1)} fusion(f32[256,128]{1,0:T(8,128)S(1)} %copy.93, pred[128,128]{1,0:T(8,128)(4,1)S(1)} %fusion.136, f32[8,256,1,128]{3,2,1,0:T(1,128)} %get-tuple-element.526, s32[]{:T(128)S(6)} %copy.104), kind=kOutput, calls=%fused_computation.2.clone.1 | convolution fusion | flops 62914560 | bytes 540676 | tf_op jit(solution)/shard_map/while/body/eval_jaxpr/cstu,csu->cst/dot_general | solution.py:111
  288.9 28.5 %fusion.137 = f32[256,1,128]{2,1,0:T(1,128)S(1)} fusion(f32[256,128]{1,0:T(8,128)S(1)} %copy.93, pred[128,128]{1,0:T(8,128)(4,1)S(1)} %fusion.136, f32[8,256,1,128]{3,2,1,0:T(1,128)} %get-tuple-element.526, s32[]{:T(128)S(6)} %copy.104), kind=kOutput, calls=%fused_computation.2.clone.1 | convolution fusion | flops 62914560 | bytes 540676 | tf_op jit(solution)/shard_map/while/body/eval_jaxpr/cstu,csu->cst/dot_general | solution.py:111
  320.0 28.5 %fusion.137 = f32[256,1,128]{2,1,0:T(1,128)S(1)} fusion(f32[256,128]{1,0:T(8,128)S(1)} %copy.93, pred[128,128]{1,0:T(8,128)(4,1)S(1)} %fusion.136, f32[8,256,1,128]{3,2,1,0:T(1,128)} %get-tuple-element.526, s32[]{:T(128)S(6)} %copy.104), kind=kOutput, calls=%fused_computation.2.clone.1 | convolution fusion | flops 62914560 | bytes 540676 | tf_op jit(solution)/shard_map/while/body/eval_jaxpr/cstu,csu->cst/dot_general | solution.py:111
  364.0 16.6 %psum.49 = f32[1024]{0:T(1024)S(1)} all-reduce(f32[1024]{0:T(1024)S(1)} %bitcast.246), channel_id=1, replica_groups=mesh['dp'=4,'mp'=8] {'mp'}, use_global_device_ids=true, to_apply=%region_7.8 | all-reduce | flops 1024 | bytes 8192 | tf_op jit(solution)/shard_map/psum | solution.py:123
  382.5 4.5 convolution_convert_fusion.3
  389.8 4.2 constant_dynamic-update-slice_fusion.4
  395.8 145.9 %all-reduce.5.cloned.1.call-done = bf16[1024,2048]{1,0:T(8,128)(2,1)} async-done(((bf16[1024,2048]{1,0:T(8,128)(2,1)}), bf16[1024,2048]{1,0:T(8,128)(2,1)}) %all-reduce.5.cloned.1.call-update) | async-done | bytes 4194320 | tf_op jit(solution)/shard_map/psum | solution.py:129
  541.7 8.2 convert_add_fusion
  549.9 11.4 fusion.92
  561.3 56.1 %all-gather.6.cloned.1.call-done = bf16[1024,2048]{1,0:T(8,128)(2,1)} async-done(((bf16[128,2048]{1,0:T(8,128)(2,1)}), bf16[1024,2048]{1,0:T(8,128)(2,1)}) %all-gather.6.cloned.1.call-update) | async-done | bytes 4194320 | tf_op jit(solution)/shard_map/all_gather | solution.py:150
  617.4 9.3 multiply_convert_fusion.2
  628.4 10.9 convolution_convert_fusion.1
  639.4 6.7 convert_multiply_fusion.2
  647.5 79.2 %reduce-scatter.9.cloned.1.call-done = bf16[128,2048]{1,0:T(8,128)(2,1)} async-done(((bf16[1024,2048]{1,0:T(8,128)(2,1)}), bf16[128,2048]{1,0:T(8,128)(2,1)}) %reduce-scatter.9.cloned.1.call-update) | async-done | bytes 524304 | tf_op jit(solution)/shard_map/reduce_scatter | solution.py:164
  731.8 7.4 convolution_convert_fusion.6
  747.4 56.4 %all-gather.8.cloned.1.call-done = bf16[1024,2048]{1,0:T(8,128)(2,1)} async-done(((bf16[128,2048]{1,0:T(8,128)(2,1)}), bf16[1024,2048]{1,0:T(8,128)(2,1)}) %all-gather.8.cloned.1.call-update) | async-done | bytes 4194320 | tf_op jit(solution)/shard_map/all_gather | solution.py:174
  803.8 5.6 multiply_reduce_fusion.1
  809.4 16.6 %psum.51 = f32[1024]{0:T(1024)S(1)} all-reduce(f32[1024]{0:T(1024)S(1)} %get-tuple-element.357), channel_id=1, replica_groups=mesh['dp'=4,'mp'=8] {'mp'}, use_global_device_ids=true, to_apply=%region_16.17 | all-reduce | flops 1024 | bytes 8192 | tf_op jit(solution)/shard_map/psum | solution.py:180
  826.0 3.5 multiply_bitcast_fusion
  835.1 182.9 %while.33 = (s32[]{:T(128)}, f32[256,1]{0,1:T(1,128)S(1)}, f32[8,256,1,128]{1,3,2,0:T(8,128)}, f32[8,256,1]{1,2,0:T(1,128)S(1)}, f32[8,1]{0,1:T(1,128)S(1)}, /*i...) while((s32[]{:T(128)}, f32[256,1]{0,1:T(1,128)S(1)}, ...), condition=%wide.region_18.19_spmd.clone.clone, body=%wide.region_17.18_spmd.clone.clone.sunk | while | flops 113853312 | bytes 2405947 | solution.py:197
  838.1 17.7 %fusion.148 = f32[256,1,128]{2,1,0:T(1,128)S(1)} fusion(f32[256,128]{1,0:T(8,128)S(1)} %copy.95, pred[128,128]{1,0:T(8,128)(4,1)S(1)} %fusion.147, f32[8,256,1,128]{3,2,1,0:T(1,128)} %get-tuple-element.557, s32[]{:T(128)S(6)} %sub.280), kind=kOutput, calls=%fused_computation.30.clone.1 | convolution fusion | flops 62914560 | bytes 540676 | tf_op jit(solution)/shard_map/while/body/eval_jaxpr/cstu,cst->csu/dot_general | solution.py:192
  861.0 17.7 %fusion.148 = f32[256,1,128]{2,1,0:T(1,128)S(1)} fusion(f32[256,128]{1,0:T(8,128)S(1)} %copy.95, pred[128,128]{1,0:T(8,128)(4,1)S(1)} %fusion.147, f32[8,256,1,128]{3,2,1,0:T(1,128)} %get-tuple-element.557, s32[]{:T(128)S(6)} %sub.280), kind=kOutput, calls=%fused_computation.30.clone.1 | convolution fusion | flops 62914560 | bytes 540676 | tf_op jit(solution)/shard_map/while/body/eval_jaxpr/cstu,cst->csu/dot_general | solution.py:192
  883.8 17.7 %fusion.148 = f32[256,1,128]{2,1,0:T(1,128)S(1)} fusion(f32[256,128]{1,0:T(8,128)S(1)} %copy.95, pred[128,128]{1,0:T(8,128)(4,1)S(1)} %fusion.147, f32[8,256,1,128]{3,2,1,0:T(1,128)} %get-tuple-element.557, s32[]{:T(128)S(6)} %sub.280), kind=kOutput, calls=%fused_computation.30.clone.1 | convolution fusion | flops 62914560 | bytes 540676 | tf_op jit(solution)/shard_map/while/body/eval_jaxpr/cstu,cst->csu/dot_general | solution.py:192
  906.6 17.7 %fusion.148 = f32[256,1,128]{2,1,0:T(1,128)S(1)} fusion(f32[256,128]{1,0:T(8,128)S(1)} %copy.95, pred[128,128]{1,0:T(8,128)(4,1)S(1)} %fusion.147, f32[8,256,1,128]{3,2,1,0:T(1,128)} %get-tuple-element.557, s32[]{:T(128)S(6)} %sub.280), kind=kOutput, calls=%fused_computation.30.clone.1 | convolution fusion | flops 62914560 | bytes 540676 | tf_op jit(solution)/shard_map/while/body/eval_jaxpr/cstu,cst->csu/dot_general | solution.py:192
  929.4 17.7 %fusion.148 = f32[256,1,128]{2,1,0:T(1,128)S(1)} fusion(f32[256,128]{1,0:T(8,128)S(1)} %copy.95, pred[128,128]{1,0:T(8,128)(4,1)S(1)} %fusion.147, f32[8,256,1,128]{3,2,1,0:T(1,128)} %get-tuple-element.557, s32[]{:T(128)S(6)} %sub.280), kind=kOutput, calls=%fused_computation.30.clone.1 | convolution fusion | flops 62914560 | bytes 540676 | tf_op jit(solution)/shard_map/while/body/eval_jaxpr/cstu,cst->csu/dot_general | solution.py:192
  952.3 17.7 %fusion.148 = f32[256,1,128]{2,1,0:T(1,128)S(1)} fusion(f32[256,128]{1,0:T(8,128)S(1)} %copy.95, pred[128,128]{1,0:T(8,128)(4,1)S(1)} %fusion.147, f32[8,256,1,128]{3,2,1,0:T(1,128)} %get-tuple-element.557, s32[]{:T(128)S(6)} %sub.280), kind=kOutput, calls=%fused_computation.30.clone.1 | convolution fusion | flops 62914560 | bytes 540676 | tf_op jit(solution)/shard_map/while/body/eval_jaxpr/cstu,cst->csu/dot_general | solution.py:192
  975.1 17.7 %fusion.148 = f32[256,1,128]{2,1,0:T(1,128)S(1)} fusion(f32[256,128]{1,0:T(8,128)S(1)} %copy.95, pred[128,128]{1,0:T(8,128)(4,1)S(1)} %fusion.147, f32[8,256,1,128]{3,2,1,0:T(1,128)} %get-tuple-element.557, s32[]{:T(128)S(6)} %sub.280), kind=kOutput, calls=%fused_computation.30.clone.1 | convolution fusion | flops 62914560 | bytes 540676 | tf_op jit(solution)/shard_map/while/body/eval_jaxpr/cstu,cst->csu/dot_general | solution.py:192
  997.9 17.7 %fusion.148 = f32[256,1,128]{2,1,0:T(1,128)S(1)} fusion(f32[256,128]{1,0:T(8,128)S(1)} %copy.95, pred[128,128]{1,0:T(8,128)(4,1)S(1)} %fusion.147, f32[8,256,1,128]{3,2,1,0:T(1,128)} %get-tuple-element.557, s32[]{:T(128)S(6)} %sub.280), kind=kOutput, calls=%fused_computation.30.clone.1 | convolution fusion | flops 62914560 | bytes 540676 | tf_op jit(solution)/shard_map/while/body/eval_jaxpr/cstu,cst->csu/dot_general | solution.py:192
  1028.5 7.0 convolution_convert_fusion.4
  1035.6 6.4 convolution_convert_fusion.2
  1042.2 13.5 convolution_convert_fusion
  1055.7 6.4 convolution_convert_fusion.5
  1062.1 9.0 pad_maximum_fusion
  1077.6 46.3 %reduce-scatter.11.cloned.1.call-done = bf16[128,2048]{1,0:T(8,128)(2,1)} async-done(((bf16[1024,2048]{1,0:T(8,128)(2,1)}), bf16[128,2048]{1,0:T(8,128)(2,1)}) %reduce-scatter.11.cloned.1.call-update) | async-done | bytes 524304 | tf_op jit(solution)/shard_map/reduce_scatter | solution.py:222
  1125.4 42.5 %all-reduce.1 = (f32[2048]{0:T(1024)}, f32[2048]{0:T(1024)}, f32[2048]{0:T(1024)}) all-reduce(f32[2048]{0:T(1024)S(1)} %get-tuple-element.358, f32[2048]{0:T(1024)S(1)} %get-tuple-element.354, f32[2048]{0:T(1024)S(1)} %mul.516), channel_id=1, replica_groups=mesh['dp'=4,'mp'=8] {'dp','mp'}, use_global_device_ids=true, to_apply=%region_22.23 | all-reduce | flops 6144 | bytes 49152 | tf_op jit(solution)/shard_map/psum | solution.py:254
  1167.8 48.6 %reduce-scatter.7.cloned.1.call-done = bf16[128,2048]{1,0:T(8,128)(2,1)} async-done(((bf16[1024,2048]{1,0:T(8,128)(2,1)}), bf16[128,2048]{1,0:T(8,128)(2,1)}) %reduce-scatter.7.cloned.1.call-update) | async-done | bytes 524304 | tf_op jit(solution)/shard_map/reduce_scatter | solution.py:140
  1216.4 3.6 fusion.64
  1220.1 72.7 %reduce-scatter.13.cloned.1.call-done = bf16[512,2176]{0,1:T(8,128)(2,1)} async-done(((bf16[2048,2176]{0,1:T(8,128)(2,1)}), bf16[512,2176]{0,1:T(8,128)(2,1)}) %reduce-scatter.13.cloned.1.call-update) | async-done | bytes 2228240 | tf_op jit(solution)/shard_map/reduce_scatter | solution.py:236
  1302.5 123.1 %all-reduce.7.cloned.1.call-done = f32[24,2048]{1,0:T(8,128)} async-done(((f32[24,2048]{1,0:T(8,128)}), f32[24,2048]{1,0:T(8,128)}) %all-reduce.7.cloned.1.call-update) | async-done | bytes 196624 | tf_op jit(solution)/shard_map/psum | solution.py:254
  (350 shorter events, 138.4 us)
Async XLA Ops:
  7.2 610.2 %copy-start = (bf16[704,2048]{1,0:T(8,128)(2,1)S(1)}, bf16[704,2048]{1,0:T(8,128)(2,1)}, u32[]{:S(2)}) copy-start(bf16[704,2048]{1,0:T(8,128)(2,1)} %param.35) | copy-start | bytes 8650756
  7.2 76.9 %all-gather.4.cloned.1.call-start = ((), (), s32[]{:S(2)}) async-start(), calls=%async_computation.6 | async-start | bytes 4718592 | tf_op jit(solution)/shard_map/all_gather | solution.py:68
  7.9 533.8 %all-reduce.5.cloned.1.call-start = ((), (), s32[]{:S(2)}) async-start(), calls=%async_computation.7 | async-start | bytes 8388608 | tf_op jit(solution)/shard_map/psum | solution.py:129
  8.8 2.6 copy-start.20
  8.8 7.4 copy-start.11
  8.8 1.7 copy-start.28
  10.6 0.9 copy-start.26
  11.4 81.7 %copy-start.24 = (f32[256]{0:T(256)}, f32[256]{0:T(256)S(1)}, u32[]{:S(2)}) copy-start(f32[256]{0:T(256)S(1)} %multiply_reduce_fusion.4) | copy-start | bytes 3076
  11.4 81.7 %copy-start.22 = (f32[256]{0:T(256)}, f32[256]{0:T(256)S(1)}, u32[]{:S(2)}) copy-start(f32[256]{0:T(256)S(1)} %broadcast_subtract_fusion.1) | copy-start | bytes 3076
  13.8 73.5 %copy-start.18 = (f32[2048]{0:T(1024)S(1)}, f32[2048]{0:T(1024)}, u32[]{:S(2)}) copy-start(f32[2048]{0:T(1024)} %param.25) | copy-start | bytes 24580
  84.1 3.4 copy-start.3
  87.5 5.6 copy-start.30
  93.1 2.4 copy-start.1
  100.1 280.5 %copy-start.32 = (f32[256]{0:T(256)S(1)}, f32[256]{0:T(256)}, u32[]{:S(2)}) copy-start(f32[256]{0:T(256)} %param.27) | copy-start | bytes 3076
  387.0 1.5 copy-start.34
  387.1 230.3 %all-gather.6.cloned.1.call-start = ((), (), s32[]{:S(2)}) async-start(), calls=%async_computation.9 | async-start | bytes 4718592 | tf_op jit(solution)/shard_map/all_gather | solution.py:150
  387.8 338.9 %reduce-scatter.9.cloned.1.call-start = ((), (), s32[]{:S(2)}) async-start(), calls=%async_computation.10 | async-start | bytes 4718592 | tf_op jit(solution)/shard_map/reduce_scatter | solution.py:164
  389.8 4.2 copy-start.10
  395.8 154.1 %copy-start.17 = (f32[2048]{0:T(1024)S(1)}, f32[2048]{0:T(1024)}, u32[]{:S(2)}) copy-start(f32[2048]{0:T(1024)} %param.26) | copy-start | bytes 24580
  541.7 8.2 copy-start.4
  541.7 8.2 copy-start.9
  626.7 1.2 copy-start.35
  626.7 1.7 copy-start.36
  639.4 164.4 %all-gather.8.cloned.1.call-start = ((), (), s32[]{:S(2)}) async-start(), calls=%async_computation.11 | async-start | bytes 4718592 | tf_op jit(solution)/shard_map/all_gather | solution.py:174
  731.4 340.9 %reduce-scatter.17.cloned.1.call-start = ((), (), s32[]{:S(2)}) async-start(), calls=%async_computation.16 | async-start | bytes 3604480 | tf_op jit(solution)/shard_map/reduce_scatter | solution.py:246
  739.3 336.5 %reduce-scatter.15.cloned.1.call-start = ((), (), s32[]{:S(2)}) async-start(), calls=%async_computation.15 | async-start | bytes 1310720 | tf_op jit(solution)/shard_map/reduce_scatter | solution.py:243
  826.0 5.7 copy-start.33
  834.0 289.9 %reduce-scatter.11.cloned.1.call-start = ((), (), s32[]{:S(2)}) async-start(), calls=%async_computation.12 | async-start | bytes 4718592 | tf_op jit(solution)/shard_map/reduce_scatter | solution.py:222
  1020.6 6.0 copy-start.23
  1023.1 3.5 copy-start.2
  1023.1 3.8 copy-start.6
  1023.1 3.9 copy-start.25
  1026.6 1.9 copy-start.15
  1027.7 0.8 copy-start.13
  1035.5 180.9 %reduce-scatter.7.cloned.1.call-start = ((), (), s32[]{:S(2)}) async-start(), calls=%async_computation.8 | async-start | bytes 4718592 | tf_op jit(solution)/shard_map/reduce_scatter | solution.py:140
  1042.0 13.6 copy-start.19
  1042.1 13.6 copy-start.31
  1042.1 250.7 %reduce-scatter.13.cloned.1.call-start = ((), (), s32[]{:S(2)}) async-start(), calls=%async_computation.14 | async-start | bytes 11141120 | tf_op jit(solution)/shard_map/reduce_scatter | solution.py:236
  1042.1 13.6 copy-start.5
  1042.1 13.6 copy-start.14
  1042.1 13.6 copy-start.16
  1071.0 1.1 copy-start.8
  1071.0 3.7 copy-start.12
  1071.0 3.7 copy-start.21
  1071.0 3.7 copy-start.27
  1071.0 3.7 copy-start.29
  1071.1 354.5 %all-reduce.7.cloned.1.call-start = ((), (), s32[]{:S(2)}) async-start(), calls=%async_computation.13 | async-start | bytes 393216 | tf_op jit(solution)/shard_map/psum | solution.py:254
  1292.8 3.5 copy-start.7
Sparse Core Ops, SparseCore 0:
  10.2 73.8 all-gather.3
  387.2 154.4 all-reduce.4
  543.8 73.4 all-gather.5
  639.5 87.1 reduce-scatter.8
  731.5 72.2 all-gather.7
  806.3 34.3 reduce-scatter.16
  843.2 24.8 reduce-scatter.14
  1035.7 88.1 reduce-scatter.10
  1127.5 88.8 reduce-scatter.6
  1219.0 73.6 reduce-scatter.12
  1299.8 125.7 all-reduce.6
where the time goes:
time: 1440 us; the launch traced here: 1430 us
  waiting for transfers between devices  697 us (48%)
  matrix products  468 us (32%)
  other arithmetic  86.1 us (6%)
  local copies, waits for them, and re-layouts  78.9 us (5%)
  blocking collectives  75.7 us (5%)
  between operations  16.1 us (1%)
    dot_general x8, matrix products, forward_step(): jnp.einsum('cstu,csu->cst', weight, update_blk, precision=HIGH)  228 us
    psum x1, waiting for transfers between devices, local(): lax.psum(partial_mix.astype(jnp.bfloat16), 'mp').astype(jnp.float32)  146 us
    dot_general x8, matrix products, backward_step(): jnp.einsum('cstu,cst->csu', weight, grad_blk, precision=HIGH)  142 us
    psum x1, waiting for transfers between devices, local(): lax.psum((attn_gain_term, mlp_gain_term, norm_full, table_full), ('dp', '...  123 us
    reduce_scatter x1, waiting for transfers between devices, local(): lax.psum_scatter(jnp.einsum('tf,df->td', piece, w_glu, preferred_element_...  79.2 us
    reduce_scatter x1, waiting for transfers between devices, local(): lax.psum_scatter(jnp.concatenate([mix_part, glu_part], axis=1).astype(jnp...  72.7 us
    all_gather x1, waiting for transfers between devices, local(): input_all = lax.all_gather(block_input, 'mp', axis=0, tiled=True)  66.8 us
    all_gather x1, waiting for transfers between devices, local(): lax.all_gather(grad_middle.astype(jnp.bfloat16), 'mp', axis=0, tiled=True)  56.4 us
  transfers between devices with their start and end apart: 11, of which 9 were waited for; matrix products, arithmetic and copies ran while one was open for 23% of the time, Pallas kernels for 0%

commit v1 on v0

--- a/solution.py
+++ b/solution.py
@@ -126,7 +126,9 @@
     act_g = jax.nn.silu(pre_g)
     gated = (unit_states * norm_gain[:, None] * act_g).astype(jnp.bfloat16)
     partial_mix = jnp.einsum("ct,cd->td", gated, w_out, preferred_element_type=jnp.float32)
-    middle_all = input_all_f + lax.psum(partial_mix.astype(jnp.bfloat16), "mp").astype(jnp.float32)
+    middle_all = input_all_f + jnp.sum(
+        lax.all_gather(partial_mix.astype(jnp.bfloat16), "mp"), axis=0
+    ).astype(jnp.float32)
     normed_two_all = (middle_all * inverse_rms(middle_all) * mlp_gain).astype(jnp.bfloat16)
     middle = lax.dynamic_slice_in_dim(middle_all, own_start, rows_dev, 0)
     own_inv2 = inverse_rms(middle)

time: 1440 us -> 1920 us (1.33)
  waiting for transfers between devices: 697 us -> 1160 us
    all_gather x0 -> x1, waiting for transfers between devices: none -> 629 us  [local(): lax.all_gather(partial_mix.astype(jnp.bfloat16), 'mp')]
    psum x1 -> x0, waiting for transfers between devices: 146 us -> none  [local(): lax.psum(partial_mix.astype(jnp.bfloat16), 'mp').astype(jnp.float32)]
  transfers between devices with their start and end apart: 11 -> 11, of which waited for: 9 -> 9; matrix products, arithmetic and copies ran while one was open for 23% -> 18% of each run, Pallas kernels for 0% -> 0%
where the time goes in v1:
time: 1920 us
  waiting for transfers between devices  1160 us (60%)
  matrix products  468 us (24%)
  other arithmetic  101 us (5%)
  local copies, waits for them, and re-layouts  77.8 us (4%)
  blocking collectives  75.6 us (4%)
    all_gather x1, waiting for transfers between devices, local(): lax.all_gather(partial_mix.astype(jnp.bfloat16), 'mp')  629 us
    dot_general x8, matrix products, forward_step(): jnp.einsum('cstu,csu->cst', weight, update_blk, precision=HIGH)  228 us
    dot_general x8, matrix products, backward_step(): jnp.einsum('cstu,cst->csu', weight, grad_blk, precision=HIGH)  142 us
    psum x1, waiting for transfers between devices, local(): lax.psum((attn_gain_term, mlp_gain_term, norm_full, table_full), ('dp', '...  123 us
    reduce_scatter x1, waiting for transfers between devices, local(): lax.psum_scatter(jnp.einsum('tf,df->td', piece, w_glu, preferred_element_...  78.8 us
    reduce_scatter x1, waiting for transfers between devices, local(): lax.psum_scatter(jnp.concatenate([mix_part, glu_part], axis=1).astype(jnp...  72.7 us
    all_gather x1, waiting for transfers between devices, local(): input_all = lax.all_gather(block_input, 'mp', axis=0, tiled=True)  66.7 us
    all_gather x1, waiting for transfers between devices, local(): lax.all_gather(grad_middle.astype(jnp.bfloat16), 'mp', axis=0, tiled=True)  56.8 us
  transfers between devices with their start and end apart: 11, of which 9 were waited for; matrix products, arithmetic and copies ran while one was open for 18% of the time, Pallas kernels for 0%

profile of v1, /device:TPU:10, one launch (start us, length us, event | category | flops | bytes accessed | tf_op | source)
XLA Modules:
  0.0 1916.5 jit_solution(16305975826141949225)
XLA Ops:
  17.4 66.7 %all-gather.6.cloned.1.call-done = bf16[1024,2048]{1,0:T(8,128)(2,1)} async-done(((bf16[128,2048]{1,0:T(8,128)(2,1)}), bf16[1024,2048]{1,0:T(8,128)(2,1)}) %all-gather.6.cloned.1.call-update) | async-done | bytes 4194320 | tf_op jit(solution)/shard_map/all_gather | solution.py:68
  87.5 5.6 fusion.61
  100.1 259.8 %while.32 = (s32[]{:T(128)}, f32[256,1]{0,1:T(1,128)S(1)}, f32[8,256,1,128]{1,3,2,0:T(8,128)}, f32[8,1,128]{2,1,0:T(1,128)S(1)}, f32[8,256,1,128]{3,2,1,0:T(1,128)}, /*index=5*/f32[8,256,1,128]{3,2,1,0:T(1,128)}, s32[]{:T(128)}) while((s32[]{:T(128)}, f32[256,1]{0,1:T(1,128)S(1)}, f32[8,256,1,128]{1,3,2,0:T(8,128)}, ...), condition=%wide.region_5.6_spmd.clone.clone, body=%wide.region_4.0_spmd.clone.clone.sunk | while | flops 113787008 | bytes 2399189 | solution.py:116
  101.9 28.5 %fusion.137 = f32[256,1,128]{2,1,0:T(1,128)S(1)} fusion(f32[256,128]{1,0:T(8,128)S(1)} %copy.93, pred[128,128]{1,0:T(8,128)(4,1)S(1)} %fusion.136, f32[8,256,1,128]{3,2,1,0:T(1,128)} %get-tuple-element.526, s32[]{:T(128)} %get-tuple-element.514), kind=kOutput, calls=%fused_computation.2.clone.1 | convolution fusion | flops 62914560 | bytes 541184 | tf_op jit(solution)/shard_map/while/body/eval_jaxpr/cstu,csu->cst/dot_general | solution.py:111
  133.1 28.5 %fusion.137 = f32[256,1,128]{2,1,0:T(1,128)S(1)} fusion(f32[256,128]{1,0:T(8,128)S(1)} %copy.93, pred[128,128]{1,0:T(8,128)(4,1)S(1)} %fusion.136, f32[8,256,1,128]{3,2,1,0:T(1,128)} %get-tuple-element.526, s32[]{:T(128)} %get-tuple-element.514), kind=kOutput, calls=%fused_computation.2.clone.1 | convolution fusion | flops 62914560 | bytes 541184 | tf_op jit(solution)/shard_map/while/body/eval_jaxpr/cstu,csu->cst/dot_general | solution.py:111
  164.2 28.5 %fusion.137 = f32[256,1,128]{2,1,0:T(1,128)S(1)} fusion(f32[256,128]{1,0:T(8,128)S(1)} %copy.93, pred[128,128]{1,0:T(8,128)(4,1)S(1)} %fusion.136, f32[8,256,1,128]{3,2,1,0:T(1,128)} %get-tuple-element.526, s32[]{:T(128)} %get-tuple-element.514), kind=kOutput, calls=%fused_computation.2.clone.1 | convolution fusion | flops 62914560 | bytes 541184 | tf_op jit(solution)/shard_map/while/body/eval_jaxpr/cstu,csu->cst/dot_general | solution.py:111
  195.4 28.5 %fusion.137 = f32[256,1,128]{2,1,0:T(1,128)S(1)} fusion(f32[256,128]{1,0:T(8,128)S(1)} %copy.93, pred[128,128]{1,0:T(8,128)(4,1)S(1)} %fusion.136, f32[8,256,1,128]{3,2,1,0:T(1,128)} %get-tuple-element.526, s32[]{:T(128)} %get-tuple-element.514), kind=kOutput, calls=%fused_computation.2.clone.1 | convolution fusion | flops 62914560 | bytes 541184 | tf_op jit(solution)/shard_map/while/body/eval_jaxpr/cstu,csu->cst/dot_general | solution.py:111
  226.5 28.5 %fusion.137 = f32[256,1,128]{2,1,0:T(1,128)S(1)} fusion(f32[256,128]{1,0:T(8,128)S(1)} %copy.93, pred[128,128]{1,0:T(8,128)(4,1)S(1)} %fusion.136, f32[8,256,1,128]{3,2,1,0:T(1,128)} %get-tuple-element.526, s32[]{:T(128)} %get-tuple-element.514), kind=kOutput, calls=%fused_computation.2.clone.1 | convolution fusion | flops 62914560 | bytes 541184 | tf_op jit(solution)/shard_map/while/body/eval_jaxpr/cstu,csu->cst/dot_general | solution.py:111
  257.7 28.5 %fusion.137 = f32[256,1,128]{2,1,0:T(1,128)S(1)} fusion(f32[256,128]{1,0:T(8,128)S(1)} %copy.93, pred[128,128]{1,0:T(8,128)(4,1)S(1)} %fusion.136, f32[8,256,1,128]{3,2,1,0:T(1,128)} %get-tuple-element.526, s32[]{:T(128)} %get-tuple-element.514), kind=kOutput, calls=%fused_computation.2.clone.1 | convolution fusion | flops 62914560 | bytes 541184 | tf_op jit(solution)/shard_map/while/body/eval_jaxpr/cstu,csu->cst/dot_general | solution.py:111
  288.8 28.5 %fusion.137 = f32[256,1,128]{2,1,0:T(1,128)S(1)} fusion(f32[256,128]{1,0:T(8,128)S(1)} %copy.93, pred[128,128]{1,0:T(8,128)(4,1)S(1)} %fusion.136, f32[8,256,1,128]{3,2,1,0:T(1,128)} %get-tuple-element.526, s32[]{:T(128)} %get-tuple-element.514), kind=kOutput, calls=%fused_computation.2.clone.1 | convolution fusion | flops 62914560 | bytes 541184 | tf_op jit(solution)/shard_map/while/body/eval_jaxpr/cstu,csu->cst/dot_general | solution.py:111
  320.0 28.5 %fusion.137 = f32[256,1,128]{2,1,0:T(1,128)S(1)} fusion(f32[256,128]{1,0:T(8,128)S(1)} %copy.93, pred[128,128]{1,0:T(8,128)(4,1)S(1)} %fusion.136, f32[8,256,1,128]{3,2,1,0:T(1,128)} %get-tuple-element.526, s32[]{:T(128)} %get-tuple-element.514), kind=kOutput, calls=%fused_computation.2.clone.1 | convolution fusion | flops 62914560 | bytes 541184 | tf_op jit(solution)/shard_map/while/body/eval_jaxpr/cstu,csu->cst/dot_general | solution.py:111
  363.8 16.6 psum.42
  382.4 4.6 convolution_convert_fusion.3
  389.7 3.9 constant_dynamic-update-slice_fusion.4
  395.4 629.4 %all-gather.12.cloned.1.call-done = bf16[8192,2048]{1,0:T(8,128)(2,1)} async-done(((bf16[1024,2048]{1,0:T(8,128)(2,1)}), bf16[8192,2048]{1,0:T(8,128)(2,1)}) %all-gather.12.cloned.1.call-update) | async-done | bytes 33554448 | tf_op jit(solution)/shard_map/all_gather | solution.py:130
  1024.8 14.6 reduce_sum.154
  1039.4 8.2 convert_add_fusion
  1047.7 11.5 fusion.92
  1059.1 40.6 %all-gather.8.cloned.1.call-done = bf16[1024,2048]{1,0:T(8,128)(2,1)} async-done(((bf16[128,2048]{1,0:T(8,128)(2,1)}), bf16[1024,2048]{1,0:T(8,128)(2,1)}) %all-gather.8.cloned.1.call-update) | async-done | bytes 4194320 | tf_op jit(solution)/shard_map/all_gather | solution.py:152
  1099.7 9.4 multiply_convert_fusion.2
  1110.8 11.0 convolution_convert_fusion.1
  1122.2 6.7 convert_multiply_fusion.2
  1130.3 78.8 %reduce-scatter.9.cloned.1.call-done = bf16[128,2048]{1,0:T(8,128)(2,1)} async-done(((bf16[1024,2048]{1,0:T(8,128)(2,1)}), bf16[128,2048]{1,0:T(8,128)(2,1)}) %reduce-scatter.9.cloned.1.call-update) | async-done | bytes 524304 | tf_op jit(solution)/shard_map/reduce_scatter | solution.py:166
  1213.8 7.5 convolution_convert_fusion.6
  1229.4 56.8 %all-gather.10.cloned.1.call-done = bf16[1024,2048]{1,0:T(8,128)(2,1)} async-done(((bf16[128,2048]{1,0:T(8,128)(2,1)}), bf16[1024,2048]{1,0:T(8,128)(2,1)}) %all-gather.10.cloned.1.call-update) | async-done | bytes 4194320 | tf_op jit(solution)/shard_map/all_gather | solution.py:176
  1286.2 5.6 multiply_reduce_fusion.1
  1291.7 16.6 psum.43
  1308.3 3.5 multiply_bitcast_fusion
  1317.4 183.2 %while.33 = (s32[]{:T(128)}, f32[256,1]{0,1:T(1,128)S(1)}, f32[8,256,1,128]{1,3,2,0:T(8,128)}, f32[8,256,1]{1,2,0:T(1,128)S(1)}, f32[8,1]{0,1:T(1,128)S(1)}, /*i...) while((s32[]{:T(128)}, f32[256,1]{0,1:T(1,128)S(1)}, ...), condition=%wide.region_18.19_spmd.clone.clone, body=%wide.region_17.18_spmd.clone.clone.sunk | while | flops 113853312 | bytes 2405939 | solution.py:199
  1319.2 17.7 fusion.148
  1342.1 17.7 fusion.148
  1364.9 17.7 fusion.148
  1387.8 17.7 fusion.148
  1410.6 17.7 fusion.148
  1433.5 17.7 fusion.148
  1456.3 17.7 fusion.148
  1479.2 17.7 fusion.148
  1511.1 6.9 convolution_convert_fusion.4
  1518.1 6.4 convolution_convert_fusion.2
  1524.6 13.5 convolution_convert_fusion
  1538.2 6.4 convolution_convert_fusion.5
  1544.6 9.0 pad_maximum_fusion
  1560.1 46.2 %reduce-scatter.11.cloned.1.call-done = bf16[128,2048]{1,0:T(8,128)(2,1)} async-done(((bf16[1024,2048]{1,0:T(8,128)(2,1)}), bf16[128,2048]{1,0:T(8,128)(2,1)}) %reduce-scatter.11.cloned.1.call-update) | async-done | bytes 524304 | tf_op jit(solution)/shard_map/reduce_scatter | solution.py:224
  1607.8 42.5 %all-reduce.1 = (f32[2048]{0:T(1024)}, f32[2048]{0:T(1024)}, f32[2048]{0:T(1024)}) all-reduce(f32[2048]{0:T(1024)S(1)} %get-tuple-element.358, f32[2048]{0:T(1024)S(1)} %get-tuple-element.354, f32[2048]{0:T(1024)S(1)} %mul.516), channel_id=1, replica_groups=mesh['dp'=4,'mp'=8] {'dp','mp'}, use_global_device_ids=true, to_apply=%region_22.23 | all-reduce | flops 6144 | bytes 49152 | tf_op jit(solution)/shard_map/psum | solution.py:256
  1650.2 48.6 %reduce-scatter.7.cloned.1.call-done = bf16[128,2048]{1,0:T(8,128)(2,1)} async-done(((bf16[1024,2048]{1,0:T(8,128)(2,1)}), bf16[128,2048]{1,0:T(8,128)(2,1)}) %reduce-scatter.7.cloned.1.call-update) | async-done | bytes 524304 | tf_op jit(solution)/shard_map/reduce_scatter | solution.py:142
  1698.8 3.6 fusion.64
  1702.5 72.7 %reduce-scatter.13.cloned.1.call-done = bf16[512,2176]{0,1:T(8,128)(2,1)} async-done(((bf16[2048,2176]{0,1:T(8,128)(2,1)}), bf16[512,2176]{0,1:T(8,128)(2,1)}) %reduce-scatter.13.cloned.1.call-update) | async-done | bytes 2228240 | tf_op jit(solution)/shard_map/reduce_scatter | solution.py:238
  1784.9 123.1 %all-reduce.4.cloned.1.call-done = f32[24,2048]{1,0:T(8,128)} async-done(((f32[24,2048]{1,0:T(8,128)}), f32[24,2048]{1,0:T(8,128)}) %all-reduce.4.cloned.1.call-update) | async-done | bytes 196624 | tf_op jit(solution)/shard_map/psum | solution.py:256
  (351 shorter events, 141.8 us)
Async XLA Ops:
  7.2 1092.5 %copy-start = (bf16[704,2048]{1,0:T(8,128)(2,1)S(1)}, bf16[704,2048]{1,0:T(8,128)(2,1)}, u32[]{:S(2)}) copy-start(bf16[704,2048]{1,0:T(8,128)(2,1)} %param.35) | copy-start | bytes 8650756
  7.2 76.9 %all-gather.6.cloned.1.call-start = ((), (), s32[]{:S(2)}) async-start(), calls=%async_computation.6 | async-start | bytes 4718592 | tf_op jit(solution)/shard_map/all_gather | solution.py:68
  7.9 1016.9 %all-gather.12.cloned.1.call-start = ((), (), s32[]{:S(2)}) async-start(), calls=%async_computation.16 | async-start | bytes 37748736 | tf_op jit(solution)/shard_map/all_gather | solution.py:130
  8.8 2.6 copy-start.20
  8.8 7.4 copy-start.11
  8.8 1.7 copy-start.28
  10.6 0.9 copy-start.26
  11.4 81.7 %copy-start.24 = (f32[256]{0:T(256)}, f32[256]{0:T(256)S(1)}, u32[]{:S(2)}) copy-start(f32[256]{0:T(256)S(1)} %multiply_reduce_fusion.4) | copy-start | bytes 3076
  11.4 81.7 %copy-start.22 = (f32[256]{0:T(256)}, f32[256]{0:T(256)S(1)}, u32[]{:S(2)}) copy-start(f32[256]{0:T(256)S(1)} %broadcast_subtract_fusion.1) | copy-start | bytes 3076
  13.8 73.5 %copy-start.18 = (f32[2048]{0:T(1024)S(1)}, f32[2048]{0:T(1024)}, u32[]{:S(2)}) copy-start(f32[2048]{0:T(1024)} %param.25) | copy-start | bytes 24580
  84.1 3.4 copy-start.4
  87.5 5.6 copy-start.30
  93.1 2.4 copy-start.1
  100.1 280.4 %copy-start.32 = (f32[256]{0:T(256)S(1)}, f32[256]{0:T(256)}, u32[]{:S(2)}) copy-start(f32[256]{0:T(256)} %param.27) | copy-start | bytes 3076
  387.0 1.5 copy-start.34
  387.0 712.7 %all-gather.8.cloned.1.call-start = ((), (), s32[]{:S(2)}) async-start(), calls=%async_computation.8 | async-start | bytes 4718592 | tf_op jit(solution)/shard_map/all_gather | solution.py:152
  387.7 821.4 %reduce-scatter.9.cloned.1.call-start = ((), (), s32[]{:S(2)}) async-start(), calls=%async_computation.9 | async-start | bytes 4718592 | tf_op jit(solution)/shard_map/reduce_scatter | solution.py:166
  389.7 3.9 copy-start.10
  1039.4 8.2 copy-start.3
  1039.4 8.2 copy-start.5
  1039.4 8.2 copy-start.17
  1109.1 1.2 copy-start.35
  1109.1 1.6 copy-start.36
  1121.7 164.4 %all-gather.10.cloned.1.call-start = ((), (), s32[]{:S(2)}) async-start(), calls=%async_computation.10 | async-start | bytes 4718592 | tf_op jit(solution)/shard_map/all_gather | solution.py:176
  1213.7 341.1 %reduce-scatter.17.cloned.1.call-start = ((), (), s32[]{:S(2)}) async-start(), calls=%async_computation.15 | async-start | bytes 3604480 | tf_op jit(solution)/shard_map/reduce_scatter | solution.py:248
  1221.3 337.0 %reduce-scatter.15.cloned.1.call-start = ((), (), s32[]{:S(2)}) async-start(), calls=%async_computation.14 | async-start | bytes 1310720 | tf_op jit(solution)/shard_map/reduce_scatter | solution.py:245
  1308.3 5.7 copy-start.33
  1316.3 290.0 %reduce-scatter.11.cloned.1.call-start = ((), (), s32[]{:S(2)}) async-start(), calls=%async_computation.11 | async-start | bytes 4718592 | tf_op jit(solution)/shard_map/reduce_scatter | solution.py:224
  1503.1 6.0 copy-start.23
  1505.7 3.5 copy-start.2
  1505.7 3.8 copy-start.7
  1505.7 3.9 copy-start.25
  1509.1 1.9 copy-start.15
  1510.3 0.8 copy-start.13
  1518.1 180.8 %reduce-scatter.7.cloned.1.call-start = ((), (), s32[]{:S(2)}) async-start(), calls=%async_computation.7 | async-start | bytes 4718592 | tf_op jit(solution)/shard_map/reduce_scatter | solution.py:142
  1524.5 13.6 copy-start.19
  1524.5 13.6 copy-start.31
  1524.5 250.6 %reduce-scatter.13.cloned.1.call-start = ((), (), s32[]{:S(2)}) async-start(), calls=%async_computation.13 | async-start | bytes 11141120 | tf_op jit(solution)/shard_map/reduce_scatter | solution.py:238
  1524.6 13.6 copy-start.6
  1524.6 13.6 copy-start.14
  1524.6 13.6 copy-start.16
  1553.5 1.1 copy-start.9
  1553.5 3.7 copy-start.12
  1553.5 3.7 copy-start.21
  1553.5 3.7 copy-start.27
  1553.5 3.7 copy-start.29
  1553.6 354.4 %all-reduce.4.cloned.1.call-start = ((), (), s32[]{:S(2)}) async-start(), calls=%async_computation.12 | async-start | bytes 393216 | tf_op jit(solution)/shard_map/psum | solution.py:256
  1775.2 3.5 copy-start.8
Sparse Core Ops, SparseCore 0:
  10.2 73.8 all-gather.5
  387.1 637.6 all-gather.11
  1026.9 72.7 all-gather.7
  1121.9 87.1 reduce-scatter.8
  1213.8 72.2 all-gather.9
  1288.7 34.3 reduce-scatter.16
  1325.6 24.8 reduce-scatter.14
  1518.2 88.0 reduce-scatter.10
  1609.9 88.8 reduce-scatter.6
  1701.5 73.6 reduce-scatter.12
  1782.2 125.7 all-reduce.3
